TPU v7x, 512 devices: a whole 4x8x8 slice. The times are simulated.
512 devices in a mesh: shell: 8 (over z), row: 4 (over x_hi, core), col: 16 (over x_lo, y).
Axes of the slice: x: 4 (x_hi: 2, x_lo: 2; x = x_hi * 2 + x_lo), y: 8, z: 8, core: 2. Of those that a mesh axis runs over, the one named last changes fastest.
Arguments:
- left_basis: bfloat16 [2, 4096, 6144], P(None, 'row', 'shell'), may hold values from -6 to 6
- right_basis: bfloat16 [2, 6144, 8192], P(None, 'shell', 'col'), may hold values from -0.078125 to 0.078125
- point_weight: float32 [6144], P('shell'), may hold values from 0.3 to 3
- shell_index: int32 [6144], P('shell'), may hold values from 0 to 11
- green_table: float32 [12, 2], replicated, may hold values from -4 to 4
- pivot_rows: int32 [512], replicated, may hold values from 0 to 4095, as said below
- diag_inverse: bfloat16 [2, 512, 512], replicated, may hold values from -0.005859375 to 0.005859375
Outputs:
- factored: float32 [2, 4, 8, 128, 8192], P(None, 'row', 'shell', None, 'col')
Inputs may be any that keep to these rules, and one draw needn't show every extreme that they name: `pivot_rows`: 512 distinct matrix rows.
All inputs are finite; a program needn't handle non-finite values.
Results may differ from a plain program's by a relative error of at most 0.0056.
Values may be sent and summed in bfloat16 or wider, within the bound.
No kernel may reach another device: no remote copies, remote signals or barrier semaphores. Data moves between devices by JAX's collectives and lax.ppermute only.
A program may use at most 128 MiB of HBM per device.

v0:
```python
import jax
import jax.numpy as jnp
from jax import lax
from jax.sharding import PartitionSpec as P


def broadcast(block, axis, source):
    block = jnp.where(lax.axis_index(axis) == source, block, jnp.zeros_like(block))
    return lax.psum(block, axis)


def complex_block(real_part, imag_part):
    upper_half = jnp.concatenate([real_part, imag_part], axis=1)
    lower_half = jnp.concatenate([-imag_part, real_part], axis=1)
    return jnp.concatenate([upper_half, lower_half], axis=0)


def weigh_points(right_basis, point_weight, shell_index, green_table):
    shells_count = green_table.shape[0]
    matches = shell_index[:, None] == jnp.arange(shells_count, dtype=jnp.int32)[None, :]
    green_real = jnp.sum(jnp.where(matches, green_table[None, :, 0], 0.0), axis=1)
    green_imag = jnp.sum(jnp.where(matches, green_table[None, :, 1], 0.0), axis=1)
    weight_real = point_weight * green_real
    weight_imag = point_weight * green_imag
    basis_real = right_basis[0].astype(jnp.float32)
    basis_imag = right_basis[1].astype(jnp.float32)
    weighted_real = (weight_real[:, None] * basis_real - weight_imag[:, None] * basis_imag).astype(
        jnp.bfloat16
    )
    weighted_imag = (weight_real[:, None] * basis_imag + weight_imag[:, None] * basis_real).astype(
        jnp.bfloat16
    )
    return (weighted_real, weighted_imag)


def reduce_tiles(term_rows, owned_rows):
    return lax.psum_scatter(
        term_rows(jnp.int32(0), owned_rows * lax.axis_size("shell")),
        "shell",
        scatter_dimension=0,
        tiled=True,
    )


def pick_rows(matrix_rows, pivot_rows, row_base):
    held_rows = matrix_rows.shape[0]
    local_index = pivot_rows - row_base
    inside = (local_index >= 0) & (local_index < held_rows)
    picked = jnp.take(matrix_rows, jnp.clip(local_index, 0, held_rows - 1), axis=0)
    return jnp.where(inside[:, None], picked, 0.0)


def select_pivots(coupling, pivot_rows, row_base):
    picked = pick_rows(coupling, pivot_rows, row_base).astype(jnp.bfloat16)
    return lax.psum(picked, ("shell", "row")).astype(jnp.float32).astype(jnp.bfloat16)


def body(left_basis, right_basis, point_weight, shell_index, green_table, pivot_rows, diag_inverse):
    shells = lax.axis_size("shell")
    owned_rows = left_basis.shape[1] // shells
    panel_width = right_basis.shape[2]
    weighted_real, weighted_imag = weigh_points(right_basis, point_weight, shell_index, green_table)
    grid_row = lax.axis_index("row")
    shell_rank = lax.axis_index("shell")
    row_base = (grid_row * shells + shell_rank) * owned_rows
    left_stack = jnp.concatenate([left_basis[0], left_basis[1]], axis=1)
    right_stack = complex_block(weighted_real, weighted_imag)

    def from_bases(first_row, row_count):
        return jnp.dot(left_stack, right_stack, preferred_element_type=jnp.float32)

    coupling = reduce_tiles(from_bases, owned_rows)
    pivot_sum = select_pivots(coupling, pivot_rows, row_base)
    panel_real = coupling[:, :panel_width]
    panel_imag = coupling[:, panel_width:]
    inverse_real = diag_inverse[0].astype(jnp.float32)
    inverse_imag = diag_inverse[1].astype(jnp.float32)
    highest = lax.Precision.HIGHEST
    mult_real = (
        jnp.dot(panel_real, inverse_real, precision=highest, preferred_element_type=jnp.float32)
        - jnp.dot(panel_imag, inverse_imag, precision=highest, preferred_element_type=jnp.float32)
    ).astype(jnp.bfloat16)
    mult_imag = (
        jnp.dot(panel_real, inverse_imag, precision=highest, preferred_element_type=jnp.float32)
        + jnp.dot(panel_imag, inverse_real, precision=highest, preferred_element_type=jnp.float32)
    ).astype(jnp.bfloat16)
    multipliers = jnp.concatenate([mult_real, mult_imag], axis=1)
    multipliers = broadcast(multipliers, "col", 0)
    pivot_block = complex_block(pivot_sum[:, :panel_width], pivot_sum[:, panel_width:])
    update = jnp.dot(multipliers, pivot_block, preferred_element_type=jnp.float32)
    updated = coupling - update
    return jnp.stack([updated[:, :panel_width], updated[:, panel_width:]]).reshape(
        2, 1, 1, owned_rows, panel_width
    )


def solution(mesh):
    return jax.shard_map(
        body,
        mesh=mesh,
        in_specs=(
            P(None, "row", "shell"),
            P(None, "shell", "col"),
            P("shell"),
            P("shell"),
            P(),
            P(),
            P(),
        ),
        out_specs=P(None, "row", "shell", None, "col"),
        check_vma=False,
    )
```

profile of v0, /device:TPU:4, one launch (start us, length us, event | category | flops | bytes accessed | tf_op | source)
XLA Modules:
  0.0 509.2 jit_solution(4400206457405959289)
XLA Ops:
  6.5 0.8 slice_bitcast_fusion.4
  7.4 0.8 select_reduce_fusion.1
  8.1 0.7 fusion.44
  8.8 1.9 fusion.42
  10.8 0.4 fusion.18
  11.2 0.2 slice_bitcast_fusion.1
  11.4 5.3 %fusion = f32[1024,1024]{1,0:T(8,128)} fusion(bf16[1024,768]{1,0:T(8,128)(2,1)S(1)} %get-tuple-element.12, bf16[1024,768]{1,0:T(8,128)(2,1)S(1)} %get-tuple-element.11, bf16[768,512]{1,0:T(8,128)(2,1)S(1)} %fusion.18, bf16[768,512]{1,0:T(8,128)(2,1)S(1)} %get-tuple-element.9, bf16[768,512]{1,0:T(8,128)(2,1)S(1)} %get-tuple-element.10), kind=kOutput, calls=%fused_computation.1 | convolution fusion | flops 3240099840 | bytes 9699328 | tf_op jit(solution)/shard_map/dot_general | solution.py:70
  16.8 0.0 all-reduce.5.cloned.1.call-start
  16.8 0.6 copy-done.5
  17.4 62.8 %reduce-scatter.2.cloned.1.call-done = f32[128,1024]{1,0:T(8,128)} async-done(((f32[1024,1024]{1,0:T(8,128)}), f32[128,1024]{1,0:T(8,128)}) %reduce-scatter.2.cloned.1.call-update) | async-done | bytes 524304 | tf_op jit(solution)/shard_map/reduce_scatter | solution.py:37
  80.3 3.8 gather_fusion
  84.1 1.4 select_convert_fusion
  85.4 0.0 all-reduce.3.cloned.1.call-start
  85.5 0.2 copy-done.2
  85.7 0.4 fusion.30
  86.1 0.4 fusion.26
  86.4 0.4 fusion.24
  86.8 0.4 fusion.25
  87.2 0.8 maximum_select_fusion
  88.0 267.2 %all-reduce.5.cloned.1.call-done = bf16[512,1024]{1,0:T(8,128)(2,1)} async-done(((bf16[512,1024]{1,0:T(8,128)(2,1)}), bf16[512,1024]{1,0:T(8,128)(2,1)}) %all-reduce.5.cloned.1.call-update) | async-done | bytes 1048592 | tf_op jit(solution)/shard_map/psum | solution.py:55
  355.2 1.4 slice_negate_fusion
  356.6 143.8 %all-reduce.3.cloned.1.call-done = bf16[128,1024]{1,0:T(8,128)(2,1)} async-done(((bf16[128,1024]{1,0:T(8,128)(2,1)}), bf16[128,1024]{1,0:T(8,128)(2,1)}) %all-reduce.3.cloned.1.call-update) | async-done | bytes 262160 | tf_op jit(solution)/shard_map/psum | solution.py:9
  500.4 1.4 fusion.21
  501.8 0.8 maximum_bitcast_fusion
  (17 shorter events, 0.1 us)
Async XLA Ops:
  6.5 4.2 copy-start.1
  6.5 73.7 %reduce-scatter.2.cloned.1.call-start = ((), (), s32[]{:S(2)}) async-start(), calls=%async_computation.1 | async-start | bytes 4718592 | tf_op jit(solution)/shard_map/reduce_scatter | solution.py:37
  8.8 2.4 copy-start.3
  16.7 0.7 copy-start.5
  16.8 338.4 %all-reduce.5.cloned.1.call-start = ((), (), s32[]{:S(2)}) async-start(), calls=%async_computation.3 | async-start | bytes 2097152 | tf_op jit(solution)/shard_map/psum | solution.py:55
  84.0 1.5 copy-start
  84.0 1.6 copy-start.2
  85.4 414.9 %all-reduce.3.cloned.1.call-start = ((), (), s32[]{:S(2)}) async-start(), calls=%async_computation.2 | async-start | bytes 524288 | tf_op jit(solution)/shard_map/psum | solution.py:9
  355.2 145.2 %copy-start.4 = (bf16[512,1024]{1,0:T(8,128)(2,1)S(1)}, bf16[512,1024]{1,0:T(8,128)(2,1)}, u32[]{:S(2)}) copy-start(bf16[512,1024]{1,0:T(8,128)(2,1)} %all-reduce.5.cloned.1.call-done) | copy-start | bytes 3145732
Sparse Core Ops, SparseCore 0:
  16.9 63.3 reduce-scatter.1
  85.6 269.6 all-reduce.4
  358.4 141.9 all-reduce.2
where the time goes:
time: 509 us
  waiting for transfers between devices  474 us (93%)
  between operations  13.2 us (3%)
  matrix products  8.23 us (2%)
  other arithmetic  8.1 us (2%)
  local copies, waits for them, and re-layouts  5.65 us (1%)
    psum x1, waiting for transfers between devices, select_pivots(): lax.psum(picked, ('shell', 'row')).astype(jnp.float32).astype(jnp.bfloat16)  267 us
    psum x1, waiting for transfers between devices, broadcast(): return lax.psum(block, axis)  144 us
    reduce_scatter x1, waiting for transfers between devices, reduce_tiles(): lax.psum_scatter(term_rows(jnp.int32(0), owned_rows * lax.axis_size('shel...  62.8 us
  transfers between devices with their start and end apart: 3, of which 3 were waited for; matrix products, arithmetic and copies ran while one was open for 1% of the time, Pallas kernels for 0%

commit v1 on v0

--- a/solution.py
+++ b/solution.py
@@ -2,6 +2,11 @@
 import jax.numpy as jnp
 from jax import lax
 from jax.sharding import PartitionSpec as P
+
+
+def axis_by_axis(array, first, second):
+    inner = lax.psum(array, first)
+    return lax.psum(inner, second)
 
 
 def broadcast(block, axis, source):
@@ -52,7 +57,7 @@
 
 def select_pivots(coupling, pivot_rows, row_base):
     picked = pick_rows(coupling, pivot_rows, row_base).astype(jnp.bfloat16)
-    return lax.psum(picked, ("shell", "row")).astype(jnp.float32).astype(jnp.bfloat16)
+    return axis_by_axis(picked, "row", "shell").astype(jnp.float32).astype(jnp.bfloat16)
 
 
 def body(left_basis, right_basis, point_weight, shell_index, green_table, pivot_rows, diag_inverse):

time: 509 us -> 373 us (0.73)
  waiting for transfers between devices: 474 us -> 338 us
    psum x1 -> x2, waiting for transfers between devices: 267 us -> 136 us  [the longest x1 84 us: axis_by_axis(): return lax.psum(inner, second)]
    psum x1, waiting for transfers between devices: 144 us -> 139 us  [broadcast(): return lax.psum(block, axis)]
  transfers between devices with their start and end apart: 3 -> 4, of which waited for: 3 -> 4; matrix products, arithmetic and copies ran while one was open for 1% -> 1% of each run, Pallas kernels for 0% -> 0%
where the time goes in v1:
time: 373 us
  waiting for transfers between devices  338 us (91%)
  between operations  13.3 us (4%)
  matrix products  8.23 us (2%)
  other arithmetic  8.1 us (2%)
  local copies, waits for them, and re-layouts  5.46 us (1%)
    psum x1, waiting for transfers between devices, broadcast(): return lax.psum(block, axis)  139 us
    psum x1, waiting for transfers between devices, axis_by_axis(): return lax.psum(inner, second)  84 us
    reduce_scatter x1, waiting for transfers between devices, reduce_tiles(): lax.psum_scatter(term_rows(jnp.int32(0), owned_rows * lax.axis_size('shel...  62.8 us
    psum x1, waiting for transfers between devices, axis_by_axis(): inner = lax.psum(array, first)  52.3 us
  transfers between devices with their start and end apart: 4, of which 4 were waited for; matrix products, arithmetic and copies ran while one was open for 1% of the time, Pallas kernels for 0%

profile of v1, /device:TPU:4, one launch (start us, length us, event | category | flops | bytes accessed | tf_op | source)
XLA Modules:
  0.0 373.0 jit_solution(9975835405656101490)
XLA Ops:
  6.5 0.8 slice_bitcast_fusion.4
  7.4 0.8 select_reduce_fusion.1
  8.1 0.7 fusion.44
  8.8 1.9 fusion.42
  10.8 0.4 fusion.18
  11.2 0.2 slice_bitcast_fusion.1
  11.4 5.3 %fusion = f32[1024,1024]{1,0:T(8,128)} fusion(bf16[1024,768]{1,0:T(8,128)(2,1)S(1)} %get-tuple-element.12, bf16[1024,768]{1,0:T(8,128)(2,1)S(1)} %get-tuple-element.11, bf16[768,512]{1,0:T(8,128)(2,1)S(1)} %fusion.18, bf16[768,512]{1,0:T(8,128)(2,1)S(1)} %get-tuple-element.9, bf16[768,512]{1,0:T(8,128)(2,1)S(1)} %get-tuple-element.10), kind=kOutput, calls=%fused_computation.1 | convolution fusion | flops 3240099840 | bytes 9699328 | tf_op jit(solution)/shard_map/dot_general | solution.py:75
  16.8 0.0 all-reduce.6.cloned.1.call-start
  16.8 0.6 copy-done.5
  17.4 62.8 %reduce-scatter.2.cloned.1.call-done = f32[128,1024]{1,0:T(8,128)} async-done(((f32[1024,1024]{1,0:T(8,128)}), f32[128,1024]{1,0:T(8,128)}) %reduce-scatter.2.cloned.1.call-update) | async-done | bytes 524304 | tf_op jit(solution)/shard_map/reduce_scatter | solution.py:42
  80.3 3.8 %gather_fusion = bf16[512,1024]{1,0:T(8,128)(2,1)S(1)} fusion(f32[128,1024]{1,0:T(8,128)} %reduce-scatter.2.cloned.1.call-done, s32[1024]{0:T(1024)S(1)} %pad_clamp_fusion), kind=kCustom, calls=%fused_computation | custom fusion | bytes 2099200 | tf_op jit(solution)/shard_map/jit(_take)/gather | solution.py:54
  84.1 1.4 select_convert_fusion
  85.4 0.0 all-reduce.8.cloned.1.call-start
  85.5 52.3 %all-reduce.6.cloned.1.call-done = bf16[512,1024]{1,0:T(8,128)(2,1)} async-done(((bf16[512,1024]{1,0:T(8,128)(2,1)}), bf16[512,1024]{1,0:T(8,128)(2,1)}) %all-reduce.6.cloned.1.call-update) | async-done | bytes 1048592 | tf_op jit(solution)/shard_map/psum | solution.py:8
  137.9 0.4 fusion.30
  138.3 0.4 fusion.26
  138.6 0.4 fusion.24
  139.0 0.4 fusion.25
  139.4 0.8 maximum_select_fusion
  140.2 84.0 %all-reduce.8.cloned.1.call-done = bf16[512,1024]{1,0:T(8,128)(2,1)} async-done(((bf16[512,1024]{1,0:T(8,128)(2,1)}), bf16[512,1024]{1,0:T(8,128)(2,1)}) %all-reduce.8.cloned.1.call-update) | async-done | bytes 1048592 | tf_op jit(solution)/shard_map/psum | solution.py:9
  224.2 1.4 slice_negate_fusion
  225.5 138.6 %all-reduce.4.cloned.1.call-done = bf16[128,1024]{1,0:T(8,128)(2,1)} async-done(((bf16[128,1024]{1,0:T(8,128)(2,1)}), bf16[128,1024]{1,0:T(8,128)(2,1)}) %all-reduce.4.cloned.1.call-update) | async-done | bytes 262160 | tf_op jit(solution)/shard_map/psum | solution.py:14
  364.1 1.4 fusion.21
  365.6 0.8 maximum_bitcast_fusion
  (20 shorter events, 0.2 us)
Async XLA Ops:
  6.5 4.2 %copy-start.1 = (bf16[2,768,512]{2,1,0:T(8,128)(2,1)S(1)}, bf16[2,768,512]{2,1,0:T(8,128)(2,1)}, u32[]{:S(2)}) copy-start(bf16[2,768,512]{2,1,0:T(8,128)(2,1)} %param.8) | copy-start | bytes 4718596
  6.5 73.7 %reduce-scatter.2.cloned.1.call-start = ((), (), s32[]{:S(2)}) async-start(), calls=%async_computation.1 | async-start | bytes 4718592 | tf_op jit(solution)/shard_map/reduce_scatter | solution.py:42
  8.8 2.4 copy-start.3
  16.7 0.7 copy-start.5
  16.8 121.0 %all-reduce.6.cloned.1.call-start = ((), (), s32[]{:S(2)}) async-start(), calls=%async_computation.3 | async-start | bytes 2097152 | tf_op jit(solution)/shard_map/psum | solution.py:8
  84.0 53.8 %copy-start = (f32[128,1024]{1,0:T(8,128)S(1)}, f32[128,1024]{1,0:T(8,128)}, u32[]{:S(2)}) copy-start(f32[128,1024]{1,0:T(8,128)} %reduce-scatter.2.cloned.1.call-done) | copy-start | bytes 1572868
  84.0 53.8 %copy-start.2 = (bf16[2,512,512]{2,1,0:T(8,128)(2,1)S(1)}, bf16[2,512,512]{2,1,0:T(8,128)(2,1)}, u32[]{:S(2)}) copy-start(bf16[2,512,512]{2,1,0:T(8,128)(2,1)} %param.13) | copy-start | bytes 3145732
  85.4 138.7 %all-reduce.8.cloned.1.call-start = ((), (), s32[]{:S(2)}) async-start(), calls=%async_computation.4 | async-start | bytes 2097152 | tf_op jit(solution)/shard_map/psum | solution.py:9
  137.8 226.3 %all-reduce.4.cloned.1.call-start = ((), (), s32[]{:S(2)}) async-start(), calls=%async_computation.2 | async-start | bytes 524288 | tf_op jit(solution)/shard_map/psum | solution.py:14
  224.2 140.0 %copy-start.4 = (bf16[512,1024]{1,0:T(8,128)(2,1)S(1)}, bf16[512,1024]{1,0:T(8,128)(2,1)}, u32[]{:S(2)}) copy-start(bf16[512,1024]{1,0:T(8,128)(2,1)} %all-reduce.8.cloned.1.call-done) | copy-start | bytes 3145732
Sparse Core Ops, SparseCore 0:
  16.9 63.3 reduce-scatter.1
  85.6 52.1 all-reduce.5
  140.3 83.8 all-reduce.7
  227.2 136.9 all-reduce.3
